TPU v7x, 32 devices: a whole 2x2x4 slice. The times are simulated.
32 devices in a mesh: seq: 8 (over z, x), tp: 4 (over y, core).
Axes of the slice: x: 2, y: 2, z: 4, core: 2. Of those that a mesh axis runs over, the one named last changes fastest.
Arguments:
- hidden_in: bfloat16 [16, 2048], replicated, may hold values from -6 to 6
- lengths: int32 [16], replicated, may hold values from 1 to 511, 2431 in all
- positions: int32 [16], replicated, may hold values from 0 to 1023
- query_weight: bfloat16 [2, 2048, 2048], P(None, 'seq', 'tp'), may hold values from -0.125 to 0.125
- key_weight: bfloat16 [2, 2048, 512], P(None, 'seq', 'tp'), may hold values from -4 to 4
- value_weight: bfloat16 [2, 2048, 512], P(None, 'seq', 'tp'), may hold values from -0.125 to 0.125
- out_weight: bfloat16 [2, 2048, 2048], P(None, 'tp', 'seq'), may hold values from -0.125 to 0.125
- gate_weight: bfloat16 [2, 2048, 8192], P(None, 'seq', 'tp'), may hold values from -0.125 to 0.125
- up_weight: bfloat16 [2, 2048, 8192], P(None, 'seq', 'tp'), may hold values from -0.125 to 0.125
- down_weight: bfloat16 [2, 8192, 2048], P(None, 'tp', 'seq'), may hold values from -0.0625 to 0.0625
- key_cache: bfloat16 [2, 16, 512, 512], P(None, None, 'seq', 'tp'), may hold values from -80 to 80
- value_cache: bfloat16 [2, 16, 512, 512], P(None, None, 'seq', 'tp'), may hold values from -6 to 6
Outputs:
- hidden_out: bfloat16 [16, 2048], replicated
- key_out: bfloat16 [2, 16, 512, 512], P(None, None, 'seq', 'tp')
- value_out: bfloat16 [2, 16, 512, 512], P(None, None, 'seq', 'tp')
Inputs may be any that keep to these rules, and one draw needn't show every extreme that they name: Request b has its cached rows at positions 0 .. lengths[b] - 1 and its new token goes to row lengths[b]; rows above are padding. The longest request has exactly 511 cached rows.
All inputs are finite; a program needn't handle non-finite values.
Results may differ from a plain program's by a relative error of at most 0.015.
Values may be sent and summed in bfloat16 or wider, within the bound.
No kernel may reach another device: no remote copies, remote signals or barrier semaphores. Data moves between devices by JAX's collectives and lax.ppermute only.
A program may use at most 64 MiB of HBM per device.

v0:
```python
import math
import jax
import jax.numpy as jnp
from jax import lax
from jax.sharding import PartitionSpec as P

HEAD_DIM = 64
LAYERS = 2
eps_norm = 1e-05
neg_fill = -1e30


def rms_norm(stream):
    as_float = stream.astype(jnp.float32)
    spread = jnp.mean(as_float * as_float, axis=-1, keepdims=True)
    return (as_float * lax.rsqrt(spread + eps_norm)).astype(jnp.bfloat16)


def rotate(heads, positions):
    half_dim = heads.shape[-1] // 2
    inverse = 500000.0 ** (-(2.0 * jnp.arange(half_dim, dtype=jnp.float32)) / heads.shape[-1])
    angles = positions.astype(jnp.float32)[:, None] * inverse[None, :]
    cosine = jnp.cos(angles)[:, None, :]
    sine = jnp.sin(angles)[:, None, :]
    first_half = heads[..., :half_dim]
    second_half = heads[..., half_dim:]
    return jnp.concatenate(
        [first_half * cosine - second_half * sine, second_half * cosine + first_half * sine],
        axis=-1,
    )


def per_device(
    hidden_in,
    lengths,
    positions,
    query_weight,
    key_weight,
    value_weight,
    out_weight,
    gate_weight,
    up_weight,
    down_weight,
    key_cache,
    value_cache,
):
    seq_index = lax.axis_index("seq")
    row_count = query_weight.shape[1]
    row_start = seq_index * row_count
    col_count = out_weight.shape[2]
    col_start = seq_index * col_count
    block_len = key_cache.shape[2]
    kv_width_here = key_cache.shape[3]
    query_width = query_weight.shape[2]
    requests = hidden_in.shape[0]
    group_heads = query_width // HEAD_DIM
    kv_here = kv_width_here // HEAD_DIM
    repeat = group_heads // kv_here
    score_scale = 1.0 / math.sqrt(HEAD_DIM)
    global_slots = seq_index * block_len + jnp.arange(block_len, dtype=jnp.int32)
    new_slot = (global_slots[None, :] == lengths[:, None])[:, :, None]
    live_mask = (global_slots[None, :] <= lengths[:, None])[:, None, None, :]

    def finish(part_terms, stream_now):
        summed = lax.psum(part_terms, "tp")
        own_cols = lax.dynamic_slice_in_dim(stream_now, col_start, col_count, 1).astype(jnp.float32)
        return lax.all_gather((own_cols + summed).astype(jnp.bfloat16), "seq", axis=1, tiled=True)

    stream = hidden_in
    key_layers = []
    value_layers = []
    for layer_idx in range(LAYERS):
        normed = rms_norm(stream)
        own_rows = lax.dynamic_slice_in_dim(normed, row_start, row_count, 1)
        query_part = jnp.dot(own_rows, query_weight[layer_idx], preferred_element_type=jnp.float32)
        key_part = jnp.dot(own_rows, key_weight[layer_idx], preferred_element_type=jnp.float32)
        value_part = jnp.dot(own_rows, value_weight[layer_idx], preferred_element_type=jnp.float32)
        query, key_new, value_new = lax.psum((query_part, key_part, value_part), "seq")
        query = rotate(query.reshape(requests, group_heads, HEAD_DIM), positions).astype(
            jnp.bfloat16
        )
        query = query.reshape(requests, kv_here, repeat, HEAD_DIM)
        key_new = (
            rotate(key_new.reshape(requests, kv_here, HEAD_DIM), positions)
            .astype(jnp.bfloat16)
            .reshape(requests, kv_width_here)
        )
        value_new = value_new.astype(jnp.bfloat16)
        key_rows = jnp.where(new_slot, key_new[:, None, :], key_cache[layer_idx])
        value_rows = jnp.where(new_slot, value_new[:, None, :], value_cache[layer_idx])
        key_heads = key_rows.reshape(requests, block_len, kv_here, HEAD_DIM)
        value_heads = value_rows.reshape(requests, block_len, kv_here, HEAD_DIM)
        scores = (
            jnp.einsum("bkrd,bskd->bkrs", query, key_heads, preferred_element_type=jnp.float32)
            * score_scale
        )
        scores = jnp.where(live_mask, scores, neg_fill)
        row_top = lax.pmax(jnp.max(scores, axis=3), "seq")
        weights = jnp.where(live_mask, jnp.exp(scores - row_top[..., None]), 0.0)
        local_sums = jnp.sum(weights, axis=3)
        local_acc = jnp.einsum(
            "bkrs,bskd->bkrd",
            weights.astype(jnp.bfloat16),
            value_heads,
            preferred_element_type=jnp.float32,
        )
        totals, weighted = lax.psum((local_sums, local_acc), "seq")
        attended = (
            (weighted / totals[..., None]).astype(jnp.bfloat16).reshape(requests, query_width)
        )
        attn_terms = jnp.dot(attended, out_weight[layer_idx], preferred_element_type=jnp.float32)
        mid = finish(attn_terms, stream)
        normed_two = rms_norm(mid)
        rows_two = lax.dynamic_slice_in_dim(normed_two, row_start, row_count, 1)
        gate_part = jnp.dot(rows_two, gate_weight[layer_idx], preferred_element_type=jnp.float32)
        up_part = jnp.dot(rows_two, up_weight[layer_idx], preferred_element_type=jnp.float32)
        gate_sum, up_sum = lax.psum((gate_part, up_part), "seq")
        hidden = (jax.nn.silu(gate_sum) * up_sum).astype(jnp.bfloat16)
        down_terms = jnp.dot(hidden, down_weight[layer_idx], preferred_element_type=jnp.float32)
        stream = finish(down_terms, mid)
        key_layers.append(key_rows)
        value_layers.append(value_rows)
    return (stream, jnp.stack(key_layers), jnp.stack(value_layers))


def solution(mesh):
    return jax.shard_map(
        per_device,
        mesh=mesh,
        in_specs=(
            P(),
            P(),
            P(),
            P(None, "seq", "tp"),
            P(None, "seq", "tp"),
            P(None, "seq", "tp"),
            P(None, "tp", "seq"),
            P(None, "seq", "tp"),
            P(None, "seq", "tp"),
            P(None, "tp", "seq"),
            P(None, None, "seq", "tp"),
            P(None, None, "seq", "tp"),
        ),
        out_specs=(P(), P(None, None, "seq", "tp"), P(None, None, "seq", "tp")),
        check_vma=False,
    )
```

profile of v0, /device:TPU:0, one launch (start us, length us, event | category | flops | bytes accessed | tf_op | source)
XLA Modules:
  0.0 562.6 jit_solution(6855281874656980006)
XLA Ops:
  13.7 39.8 %all-reduce.3 = (bf16[16,128]{1,0:T(8,128)(2,1)S(1)}, f32[16,2,64]{2,1,0:T(2,128)S(1)}, f32[16,8,64]{2,1,0:T(8,128)S(1)}) all-reduce(f32[16,128]{1,0:T(8,128)S(1)} %fusion.46, f32[16,2,64]{2,1,0:T(2,128)S(1)} %reshape.206, f32[16,8,64]{2,1,0:T(8,128)S(1)} %reshape.205), channel_id=1, replica_groups=mesh['seq'=8,'tp'=4] {'seq'}, use_global_device_ids=true, to_apply=%region_5.6 | all-reduce | flops 12288 | bytes 94208 | tf_op jit(solution)/shard_map/psum | solution.py:78
  55.8 1.7 fusion.88
  57.5 33.0 %pmax.14 = f32[16,2,4]{2,1,0:T(2,128)S(1)} all-reduce(f32[16,2,4]{2,1,0:T(2,128)S(1)} %get-tuple-element.38), channel_id=1, replica_groups=mesh['seq'=8,'tp'=4] {'seq'}, use_global_device_ids=true, to_apply=%region_4.5 | all-reduce | flops 128 | bytes 1024 | tf_op jit(solution)/shard_map/pmax | solution.py:98
  91.8 33.8 %all-reduce.2 = (f32[16,2,4,64]{3,2,1,0:T(4,128)S(1)}, f32[16,2,4]{2,1,0:T(2,128)S(1)}) all-reduce(f32[16,2,4,64]{3,2,1,0:T(4,128)S(1)} %fusion.21, f32[16,2,4]{2,1,0:T(2,128)S(1)} %fusion.56), channel_id=1, replica_groups=mesh['seq'=8,'tp'=4] {'seq'}, use_global_device_ids=true, to_apply=%region_6.7 | all-reduce | flops 8320 | bytes 66560 | tf_op jit(solution)/shard_map/psum | solution.py:107
  126.0 10.1 %psum.131 = f32[16,256]{1,0:T(8,128)S(1)} all-reduce(f32[16,256]{1,0:T(8,128)S(1)} %fusion.30), channel_id=1, replica_groups=mesh['seq'=8,'tp'=4] {'tp'}, use_global_device_ids=true, to_apply=%region_9.10 | all-reduce | flops 4096 | bytes 32768 | tf_op jit(solution)/shard_map/psum | solution.py:65
  136.8 30.5 %all_gather.12 = bf16[16,2048]{1,0:T(8,128)(2,1)S(1)} all-gather(bf16[16,256]{1,0:T(8,128)(2,1)S(1)} %add_convert_fusion.5), channel_id=1, replica_groups=mesh['seq'=8,'tp'=4] {'seq'}, dimensions={1}, use_global_device_ids=true | all-gather | bytes 73728 | tf_op jit(solution)/shard_map/all_gather | solution.py:67
  168.4 2.3 fusion.12
  171.4 69.2 %all-reduce.11.cloned.1.call-done = (f32[16,2048]{1,0:T(8,128)}, f32[16,2048]{1,0:T(8,128)}) async-done(((f32[16,2048]{1,0:T(8,128)}, f32[16,2048]{1,0:T(8,128)}), (f32[16,2048]{1,0:T(8,128)}, f32[16,2048]{1,0:T(8,128)})) %all-reduce.11.cloned.1.call-update) | async-done | bytes 262160 | tf_op jit(solution)/shard_map/psum | solution.py:117
  240.6 1.6 fusion.8
  242.2 10.1 %psum.134 = f32[16,256]{1,0:T(8,128)S(1)} all-reduce(f32[16,256]{1,0:T(8,128)S(1)} %fusion.8), channel_id=1, replica_groups=mesh['seq'=8,'tp'=4] {'tp'}, use_global_device_ids=true, to_apply=%region_13.14 | all-reduce | flops 4096 | bytes 32768 | tf_op jit(solution)/shard_map/psum | solution.py:65
  252.3 30.5 %all_gather.13 = bf16[16,2048]{1,0:T(8,128)(2,1)S(1)} all-gather(bf16[16,256]{1,0:T(8,128)(2,1)S(1)} %add_convert_fusion.4), channel_id=1, replica_groups=mesh['seq'=8,'tp'=4] {'seq'}, dimensions={1}, use_global_device_ids=true | all-gather | bytes 73728 | tf_op jit(solution)/shard_map/all_gather | solution.py:67
  286.4 36.4 %all-reduce.1 = (bf16[16,128]{1,0:T(8,128)(2,1)S(1)}, f32[16,2,64]{2,1,0:T(2,128)S(1)}, f32[16,8,64]{2,1,0:T(8,128)S(1)}) all-reduce(f32[16,128]{1,0:T(8,128)S(1)} %fusion.42, f32[16,2,64]{2,1,0:T(2,128)S(1)} %reshape.209, f32[16,8,64]{2,1,0:T(8,128)S(1)} %reshape.208), channel_id=1, replica_groups=mesh['seq'=8,'tp'=4] {'seq'}, use_global_device_ids=true, to_apply=%region_19.20 | all-reduce | flops 12288 | bytes 94208 | tf_op jit(solution)/shard_map/psum | solution.py:78
  324.4 1.9 broadcast_select_fusion.1
  326.2 1.2 squeeze.67
  327.8 1.2 fusion.89
  329.0 33.0 %pmax.15 = f32[16,2,4]{2,1,0:T(2,128)S(1)} all-reduce(f32[16,2,4]{2,1,0:T(2,128)S(1)} %get-tuple-element.40), channel_id=1, replica_groups=mesh['seq'=8,'tp'=4] {'seq'}, use_global_device_ids=true, to_apply=%region_18.19 | all-reduce | flops 128 | bytes 1024 | tf_op jit(solution)/shard_map/pmax | solution.py:98
  364.0 34.0 %all-reduce = (f32[16,2,4,64]{3,2,1,0:T(4,128)S(1)}, f32[16,2,4]{2,1,0:T(2,128)S(1)}) all-reduce(f32[16,2,4,64]{3,2,1,0:T(4,128)S(1)} %fusion.20, f32[16,2,4]{2,1,0:T(2,128)S(1)} %fusion.58), channel_id=1, replica_groups=mesh['seq'=8,'tp'=4] {'seq'}, use_global_device_ids=true, to_apply=%region_20.21 | all-reduce | flops 8320 | bytes 66560 | tf_op jit(solution)/shard_map/psum | solution.py:107
  399.3 10.1 %psum.140 = f32[16,256]{1,0:T(8,128)S(1)} all-reduce(f32[16,256]{1,0:T(8,128)S(1)} %fusion.26), channel_id=1, replica_groups=mesh['seq'=8,'tp'=4] {'tp'}, use_global_device_ids=true, to_apply=%region_23.24 | all-reduce | flops 4096 | bytes 32768 | tf_op jit(solution)/shard_map/psum | solution.py:65
  409.4 30.5 %all_gather.14 = bf16[16,2048]{1,0:T(8,128)(2,1)S(1)} all-gather(bf16[16,256]{1,0:T(8,128)(2,1)S(1)} %add_convert_fusion.3), channel_id=1, replica_groups=mesh['seq'=8,'tp'=4] {'seq'}, dimensions={1}, use_global_device_ids=true | all-gather | bytes 73728 | tf_op jit(solution)/shard_map/all_gather | solution.py:67
  441.0 2.3 fusion.6
  444.4 68.8 %all-reduce.9.cloned.1.call-done = (f32[16,2048]{1,0:T(8,128)}, f32[16,2048]{1,0:T(8,128)}) async-done(((f32[16,2048]{1,0:T(8,128)}, f32[16,2048]{1,0:T(8,128)}), (f32[16,2048]{1,0:T(8,128)}, f32[16,2048]{1,0:T(8,128)})) %all-reduce.9.cloned.1.call-update) | async-done | bytes 262160 | tf_op jit(solution)/shard_map/psum | solution.py:117
  513.3 1.2 fusion.2
  514.5 10.1 %psum.143 = f32[16,256]{1,0:T(8,128)S(1)} all-reduce(f32[16,256]{1,0:T(8,128)S(1)} %fusion.2), channel_id=1, replica_groups=mesh['seq'=8,'tp'=4] {'tp'}, use_global_device_ids=true, to_apply=%region_27.28 | all-reduce | flops 4096 | bytes 32768 | tf_op jit(solution)/shard_map/psum | solution.py:65
  524.6 30.5 %all_gather.15 = bf16[16,2048]{1,0:T(8,128)(2,1)S(1)} all-gather(bf16[16,256]{1,0:T(8,128)(2,1)S(1)} %add_convert_fusion.2), channel_id=1, replica_groups=mesh['seq'=8,'tp'=4] {'seq'}, dimensions={1}, use_global_device_ids=true | all-gather | bytes 73728 | tf_op jit(solution)/shard_map/all_gather | solution.py:67
  (97 shorter events, 24.3 us)
Async XLA Ops:
  7.2 47.1 %slice-start = ((bf16[2,16,64,128]{3,2,1,0:T(8,128)(2,1)}), bf16[1,16,64,128]{3,2,1,0:T(8,128)(2,1)S(1)}, s32[]{:S(2)}) async-start(bf16[2,16,64,128]{3,2,1,0:T(8,128)(2,1)} %param.22), calls=%async_computation.2 | async-start | bytes 524288 | tf_op jit(solution)/shard_map/slice | solution.py:89
  7.2 48.1 %copy-start.15 = (s32[16]{0:T(128)S(1)}, s32[16]{0:T(128)}, u32[]{:S(2)}) copy-start(s32[16]{0:T(128)} %param.14) | copy-start | bytes 196
  7.2 48.5 %copy-start.13 = (s32[16]{0:T(128)S(1)}, s32[16]{0:T(128)}, u32[]{:S(2)}) copy-start(s32[16]{0:T(128)} %param.13) | copy-start | bytes 196
  7.2 233.4 %all-reduce.11.cloned.1.call-start = ((), (), s32[]{:S(2)}) async-start(), calls=%async_computation.1 | async-start | bytes 524288 | tf_op jit(solution)/shard_map/psum | solution.py:117
  53.6 0.7 copy-start.10
  54.3 71.6 %copy-start.7 = (bf16[2,512,256]{2,1,0:T(8,128)(2,1)S(1)}, bf16[2,512,256]{2,1,0:T(8,128)(2,1)}, u32[]{:S(2)}) copy-start(bf16[2,512,256]{2,1,0:T(8,128)(2,1)} %param.18) | copy-start | bytes 1572868
  55.5 111.9 %copy-start = (bf16[2,256,2048]{2,1,0:T(8,128)(2,1)S(1)}, bf16[2,256,2048]{2,1,0:T(8,128)(2,1)}, u32[]{:S(2)}) copy-start(bf16[2,256,2048]{2,1,0:T(8,128)(2,1)} %param.20) | copy-start | bytes 6291460
  55.7 112.7 %copy-start.9 = (pred[16,64]{1,0:T(8,128)(4,1)}, pred[16,64]{1,0:T(8,128)(4,1)S(1)}, u32[]{:S(2)}) copy-start(pred[16,64]{1,0:T(8,128)(4,1)S(1)} %get-tuple-element.34) | copy-start | bytes 3076
  55.7 112.7 %copy-start.12 = (pred[16,64]{1,0:T(8,128)(4,1)}, pred[16,64]{1,0:T(8,128)(4,1)S(1)}, u32[]{:S(2)}) copy-start(pred[16,64]{1,0:T(8,128)(4,1)S(1)} %get-tuple-element.35) | copy-start | bytes 3076
  168.4 155.9 %copy-start.1 = (bf16[2,16,64,128]{3,2,1,0:T(8,128)(2,1)S(1)}, bf16[2,16,64,128]{3,2,1,0:T(8,128)(2,1)}, u32[]{:S(2)}) copy-start(bf16[2,16,64,128]{3,2,1,0:T(8,128)(2,1)} %param.23) | copy-start | bytes 1572868
  168.4 155.9 %copy-start.2 = (bf16[2,16,64,128]{3,2,1,0:T(8,128)(2,1)S(1)}, bf16[2,16,64,128]{3,2,1,0:T(8,128)(2,1)}, u32[]{:S(2)}) copy-start(bf16[2,16,64,128]{3,2,1,0:T(8,128)(2,1)} %param.22) | copy-start | bytes 1572868
  170.7 342.6 %all-reduce.9.cloned.1.call-start = ((), (), s32[]{:S(2)}) async-start(), calls=%async_computation | async-start | bytes 524288 | tf_op jit(solution)/shard_map/psum | solution.py:117
  322.8 0.9 copy-start.11
  323.0 0.7 copy-start.8
  364.0 79.4 %copy-start.3 = (bf16[1,16,64,128]{3,2,1,0:T(8,128)(2,1)S(1)}, bf16[1,16,64,128]{3,2,1,0:T(8,128)(2,1)}, u32[]{:S(2)}) copy-start(bf16[1,16,64,128]{3,2,1,0:T(8,128)(2,1)} %get-tuple-element.17) | copy-start | bytes 786436
  364.0 79.4 %copy-start.4 = (bf16[1,16,64,128]{3,2,1,0:T(8,128)(2,1)S(1)}, bf16[1,16,64,128]{3,2,1,0:T(8,128)(2,1)}, u32[]{:S(2)}) copy-start(bf16[1,16,64,128]{3,2,1,0:T(8,128)(2,1)} %get-tuple-element.18) | copy-start | bytes 786436
  364.0 79.4 %copy-start.5 = (bf16[1,16,64,128]{3,2,1,0:T(8,128)(2,1)S(1)}, bf16[1,16,64,128]{3,2,1,0:T(8,128)(2,1)}, u32[]{:S(2)}) copy-start(bf16[1,16,64,128]{3,2,1,0:T(8,128)(2,1)} %get-tuple-element.32) | copy-start | bytes 786436
  364.0 79.4 %copy-start.6 = (bf16[1,16,64,128]{3,2,1,0:T(8,128)(2,1)S(1)}, bf16[1,16,64,128]{3,2,1,0:T(8,128)(2,1)}, u32[]{:S(2)}) copy-start(bf16[1,16,64,128]{3,2,1,0:T(8,128)(2,1)} %get-tuple-element.33) | copy-start | bytes 786436
  441.0 72.3 %copy-start.14 = (bf16[2,2048,256]{2,1,0:T(8,128)(2,1)S(1)}, bf16[2,2048,256]{2,1,0:T(8,128)(2,1)}, u32[]{:S(2)}) copy-start(bf16[2,2048,256]{2,1,0:T(8,128)(2,1)} %param.21) | copy-start | bytes 6291460
Sparse Core Ops, SparseCore 0:
  170.8 69.7 all-reduce.10
  443.5 69.7 all-reduce.8
where the time goes:
time: 564 us; the launch traced here: 563 us
  blocking collectives  372 us (66%)
  waiting for transfers between devices  138 us (24%)
  matrix products  22 us (4%)
  between operations  14.4 us (3%)
  other arithmetic  8.02 us (1%)
  local copies, waits for them, and re-layouts  7.62 us (1%)
    psum x2, waiting for transfers between devices, per_device(): gate_sum, up_sum = lax.psum((gate_part, up_part), 'seq')  138 us
    all_gather x4, blocking collectives, finish(): lax.all_gather((own_cols + summed).astype(jnp.bfloat16), 'seq', axis=1, t...  122 us
    psum x2, blocking collectives, per_device(): lax.psum((query_part, key_part, value_part), 'seq')  76.3 us
    psum x2, blocking collectives, per_device(): totals, weighted = lax.psum((local_sums, local_acc), 'seq')  67.8 us
    pmax x2, blocking collectives, per_device(): row_top = lax.pmax(jnp.max(scores, axis=3), 'seq')  66 us
    psum x4, blocking collectives, finish(): summed = lax.psum(part_terms, 'tp')  40.5 us
  transfers between devices with their start and end apart: 2, of which 2 were waited for; matrix products, arithmetic and copies ran while one was open for 0% of the time, Pallas kernels for 0%

commit v1 on v0

--- a/solution.py
+++ b/solution.py
@@ -62,7 +62,8 @@
     live_mask = (global_slots[None, :] <= lengths[:, None])[:, None, None, :]
 
     def finish(part_terms, stream_now):
-        summed = lax.psum(part_terms, "tp")
+        z2 = lax.all_gather(part_terms, "tp")
+        summed = jnp.sum(z2, axis=0)
         own_cols = lax.dynamic_slice_in_dim(stream_now, col_start, col_count, 1).astype(jnp.float32)
         return lax.all_gather((own_cols + summed).astype(jnp.bfloat16), "seq", axis=1, tiled=True)
 

time: 564 us -> 544 us (0.965)
  blocking collectives: 372 us -> 353 us
    psum x4 -> x0, blocking collectives: 40.5 us -> none  [finish(): summed = lax.psum(part_terms, 'tp')]
    all_gather x0 -> x4, blocking collectives: none -> 21 us  [finish(): z2 = lax.all_gather(part_terms, 'tp')]
where the time goes in v1:
time: 544 us; the launch traced here: 543 us
  blocking collectives  353 us (65%)
  waiting for transfers between devices  138 us (25%)
  matrix products  22 us (4%)
  between operations  14.4 us (3%)
  other arithmetic  8.05 us (1%)
  local copies, waits for them, and re-layouts  7.62 us (1%)
    psum x2, waiting for transfers between devices, per_device(): gate_sum, up_sum = lax.psum((gate_part, up_part), 'seq')  138 us
    all_gather x4, blocking collectives, finish(): lax.all_gather((own_cols + summed).astype(jnp.bfloat16), 'seq', axis=1, t...  122 us
    psum x2, blocking collectives, per_device(): lax.psum((query_part, key_part, value_part), 'seq')  76.3 us
    psum x2, blocking collectives, per_device(): totals, weighted = lax.psum((local_sums, local_acc), 'seq')  67.8 us
    pmax x2, blocking collectives, per_device(): row_top = lax.pmax(jnp.max(scores, axis=3), 'seq')  66 us
    all_gather x4, blocking collectives, finish(): z2 = lax.all_gather(part_terms, 'tp')  21 us
  transfers between devices with their start and end apart: 2, of which 2 were waited for; matrix products, arithmetic and copies ran while one was open for 0% of the time, Pallas kernels for 0%

profile of v1, /device:TPU:0, one launch (start us, length us, event | category | flops | bytes accessed | tf_op | source)
XLA Modules:
  0.0 542.9 jit_solution(15853808710176687632)
XLA Ops:
  13.7 39.8 %all-reduce.3 = (bf16[16,128]{1,0:T(8,128)(2,1)S(1)}, f32[16,2,64]{2,1,0:T(2,128)S(1)}, f32[16,8,64]{2,1,0:T(8,128)S(1)}) all-reduce(f32[16,128]{1,0:T(8,128)S(1)} %fusion.46, f32[16,2,64]{2,1,0:T(2,128)S(1)} %reshape.206, f32[16,8,64]{2,1,0:T(8,128)S(1)} %reshape.205), channel_id=1, replica_groups=mesh['seq'=8,'tp'=4] {'seq'}, use_global_device_ids=true, to_apply=%region_5.6 | all-reduce | flops 12288 | bytes 94208 | tf_op jit(solution)/shard_map/psum | solution.py:79
  55.8 1.7 fusion.88
  57.5 33.0 %pmax.14 = f32[16,2,4]{2,1,0:T(2,128)S(1)} all-reduce(f32[16,2,4]{2,1,0:T(2,128)S(1)} %get-tuple-element.38), channel_id=1, replica_groups=mesh['seq'=8,'tp'=4] {'seq'}, use_global_device_ids=true, to_apply=%region_4.5 | all-reduce | flops 128 | bytes 1024 | tf_op jit(solution)/shard_map/pmax | solution.py:99
  91.8 33.8 %all-reduce.2 = (f32[16,2,4,64]{3,2,1,0:T(4,128)S(1)}, f32[16,2,4]{2,1,0:T(2,128)S(1)}) all-reduce(f32[16,2,4,64]{3,2,1,0:T(4,128)S(1)} %fusion.21, f32[16,2,4]{2,1,0:T(2,128)S(1)} %fusion.56), channel_id=1, replica_groups=mesh['seq'=8,'tp'=4] {'seq'}, use_global_device_ids=true, to_apply=%region_6.7 | all-reduce | flops 8320 | bytes 66560 | tf_op jit(solution)/shard_map/psum | solution.py:108
  126.0 5.2 all-gather
  131.9 30.5 %all_gather.38 = bf16[16,2048]{1,0:T(8,128)(2,1)S(1)} all-gather(bf16[16,256]{1,0:T(8,128)(2,1)S(1)} %add_convert_fusion.5), channel_id=1, replica_groups=mesh['seq'=8,'tp'=4] {'seq'}, dimensions={1}, use_global_device_ids=true | all-gather | bytes 73728 | tf_op jit(solution)/shard_map/all_gather | solution.py:68
  163.6 2.3 fusion.12
  166.6 69.1 %all-reduce.11.cloned.1.call-done = (f32[16,2048]{1,0:T(8,128)}, f32[16,2048]{1,0:T(8,128)}) async-done(((f32[16,2048]{1,0:T(8,128)}, f32[16,2048]{1,0:T(8,128)}), (f32[16,2048]{1,0:T(8,128)}, f32[16,2048]{1,0:T(8,128)})) %all-reduce.11.cloned.1.call-update) | async-done | bytes 262160 | tf_op jit(solution)/shard_map/psum | solution.py:118
  235.7 1.6 fusion.8
  237.3 5.2 all-gather.1
  242.5 30.5 %all_gather.41 = bf16[16,2048]{1,0:T(8,128)(2,1)S(1)} all-gather(bf16[16,256]{1,0:T(8,128)(2,1)S(1)} %add_convert_fusion.4), channel_id=1, replica_groups=mesh['seq'=8,'tp'=4] {'seq'}, dimensions={1}, use_global_device_ids=true | all-gather | bytes 73728 | tf_op jit(solution)/shard_map/all_gather | solution.py:68
  276.5 36.5 %all-reduce.1 = (bf16[16,128]{1,0:T(8,128)(2,1)S(1)}, f32[16,2,64]{2,1,0:T(2,128)S(1)}, f32[16,8,64]{2,1,0:T(8,128)S(1)}) all-reduce(f32[16,128]{1,0:T(8,128)S(1)} %fusion.42, f32[16,2,64]{2,1,0:T(2,128)S(1)} %reshape.209, f32[16,8,64]{2,1,0:T(8,128)S(1)} %reshape.208), channel_id=1, replica_groups=mesh['seq'=8,'tp'=4] {'seq'}, use_global_device_ids=true, to_apply=%region_19.20 | all-reduce | flops 12288 | bytes 94208 | tf_op jit(solution)/shard_map/psum | solution.py:79
  314.6 1.9 broadcast_select_fusion.1
  316.5 1.2 squeeze.67
  318.0 1.2 fusion.89
  319.3 33.0 %pmax.15 = f32[16,2,4]{2,1,0:T(2,128)S(1)} all-reduce(f32[16,2,4]{2,1,0:T(2,128)S(1)} %get-tuple-element.40), channel_id=1, replica_groups=mesh['seq'=8,'tp'=4] {'seq'}, use_global_device_ids=true, to_apply=%region_18.19 | all-reduce | flops 128 | bytes 1024 | tf_op jit(solution)/shard_map/pmax | solution.py:99
  354.2 34.0 %all-reduce = (f32[16,2,4,64]{3,2,1,0:T(4,128)S(1)}, f32[16,2,4]{2,1,0:T(2,128)S(1)}) all-reduce(f32[16,2,4,64]{3,2,1,0:T(4,128)S(1)} %fusion.20, f32[16,2,4]{2,1,0:T(2,128)S(1)} %fusion.58), channel_id=1, replica_groups=mesh['seq'=8,'tp'=4] {'seq'}, use_global_device_ids=true, to_apply=%region_20.21 | all-reduce | flops 8320 | bytes 66560 | tf_op jit(solution)/shard_map/psum | solution.py:108
  389.5 5.2 all-gather.2
  394.8 30.5 %all_gather.44 = bf16[16,2048]{1,0:T(8,128)(2,1)S(1)} all-gather(bf16[16,256]{1,0:T(8,128)(2,1)S(1)} %add_convert_fusion.3), channel_id=1, replica_groups=mesh['seq'=8,'tp'=4] {'seq'}, dimensions={1}, use_global_device_ids=true | all-gather | bytes 73728 | tf_op jit(solution)/shard_map/all_gather | solution.py:68
  426.4 2.3 fusion.6
  429.8 68.7 %all-reduce.9.cloned.1.call-done = (f32[16,2048]{1,0:T(8,128)}, f32[16,2048]{1,0:T(8,128)}) async-done(((f32[16,2048]{1,0:T(8,128)}, f32[16,2048]{1,0:T(8,128)}), (f32[16,2048]{1,0:T(8,128)}, f32[16,2048]{1,0:T(8,128)})) %all-reduce.9.cloned.1.call-update) | async-done | bytes 262160 | tf_op jit(solution)/shard_map/psum | solution.py:118
  498.5 1.2 fusion.2
  499.7 5.2 all-gather.3
  504.9 30.5 %all_gather.47 = bf16[16,2048]{1,0:T(8,128)(2,1)S(1)} all-gather(bf16[16,256]{1,0:T(8,128)(2,1)S(1)} %add_convert_fusion.2), channel_id=1, replica_groups=mesh['seq'=8,'tp'=4] {'seq'}, dimensions={1}, use_global_device_ids=true | all-gather | bytes 73728 | tf_op jit(solution)/shard_map/all_gather | solution.py:68
  (101 shorter events, 24.3 us)
Async XLA Ops:
  7.2 47.1 %slice-start = ((bf16[2,16,64,128]{3,2,1,0:T(8,128)(2,1)}), bf16[1,16,64,128]{3,2,1,0:T(8,128)(2,1)S(1)}, s32[]{:S(2)}) async-start(bf16[2,16,64,128]{3,2,1,0:T(8,128)(2,1)} %param.22), calls=%async_computation.2 | async-start | bytes 524288 | tf_op jit(solution)/shard_map/slice | solution.py:90
  7.2 48.1 %copy-start.15 = (s32[16]{0:T(128)S(1)}, s32[16]{0:T(128)}, u32[]{:S(2)}) copy-start(s32[16]{0:T(128)} %param.14) | copy-start | bytes 196
  7.2 48.5 %copy-start.13 = (s32[16]{0:T(128)S(1)}, s32[16]{0:T(128)}, u32[]{:S(2)}) copy-start(s32[16]{0:T(128)} %param.13) | copy-start | bytes 196
  7.2 228.5 %all-reduce.11.cloned.1.call-start = ((), (), s32[]{:S(2)}) async-start(), calls=%async_computation.1 | async-start | bytes 524288 | tf_op jit(solution)/shard_map/psum | solution.py:118
  53.6 0.7 copy-start.10
  54.3 71.6 %copy-start.7 = (bf16[2,512,256]{2,1,0:T(8,128)(2,1)S(1)}, bf16[2,512,256]{2,1,0:T(8,128)(2,1)}, u32[]{:S(2)}) copy-start(bf16[2,512,256]{2,1,0:T(8,128)(2,1)} %param.18) | copy-start | bytes 1572868
  55.5 107.1 %copy-start = (bf16[2,256,2048]{2,1,0:T(8,128)(2,1)S(1)}, bf16[2,256,2048]{2,1,0:T(8,128)(2,1)}, u32[]{:S(2)}) copy-start(bf16[2,256,2048]{2,1,0:T(8,128)(2,1)} %param.20) | copy-start | bytes 6291460
  55.7 107.8 %copy-start.9 = (pred[16,64]{1,0:T(8,128)(4,1)}, pred[16,64]{1,0:T(8,128)(4,1)S(1)}, u32[]{:S(2)}) copy-start(pred[16,64]{1,0:T(8,128)(4,1)S(1)} %get-tuple-element.34) | copy-start | bytes 3076
  55.7 107.8 %copy-start.12 = (pred[16,64]{1,0:T(8,128)(4,1)}, pred[16,64]{1,0:T(8,128)(4,1)S(1)}, u32[]{:S(2)}) copy-start(pred[16,64]{1,0:T(8,128)(4,1)S(1)} %get-tuple-element.35) | copy-start | bytes 3076
  163.6 151.0 %copy-start.1 = (bf16[2,16,64,128]{3,2,1,0:T(8,128)(2,1)S(1)}, bf16[2,16,64,128]{3,2,1,0:T(8,128)(2,1)}, u32[]{:S(2)}) copy-start(bf16[2,16,64,128]{3,2,1,0:T(8,128)(2,1)} %param.23) | copy-start | bytes 1572868
  163.6 151.0 %copy-start.2 = (bf16[2,16,64,128]{3,2,1,0:T(8,128)(2,1)S(1)}, bf16[2,16,64,128]{3,2,1,0:T(8,128)(2,1)}, u32[]{:S(2)}) copy-start(bf16[2,16,64,128]{3,2,1,0:T(8,128)(2,1)} %param.22) | copy-start | bytes 1572868
  165.9 332.6 %all-reduce.9.cloned.1.call-start = ((), (), s32[]{:S(2)}) async-start(), calls=%async_computation | async-start | bytes 524288 | tf_op jit(solution)/shard_map/psum | solution.py:118
  313.0 0.9 copy-start.11
  313.2 0.7 copy-start.8
  354.2 74.5 %copy-start.3 = (bf16[1,16,64,128]{3,2,1,0:T(8,128)(2,1)S(1)}, bf16[1,16,64,128]{3,2,1,0:T(8,128)(2,1)}, u32[]{:S(2)}) copy-start(bf16[1,16,64,128]{3,2,1,0:T(8,128)(2,1)} %get-tuple-element.17) | copy-start | bytes 786436
  354.2 74.5 %copy-start.4 = (bf16[1,16,64,128]{3,2,1,0:T(8,128)(2,1)S(1)}, bf16[1,16,64,128]{3,2,1,0:T(8,128)(2,1)}, u32[]{:S(2)}) copy-start(bf16[1,16,64,128]{3,2,1,0:T(8,128)(2,1)} %get-tuple-element.18) | copy-start | bytes 786436
  354.2 74.6 %copy-start.5 = (bf16[1,16,64,128]{3,2,1,0:T(8,128)(2,1)S(1)}, bf16[1,16,64,128]{3,2,1,0:T(8,128)(2,1)}, u32[]{:S(2)}) copy-start(bf16[1,16,64,128]{3,2,1,0:T(8,128)(2,1)} %get-tuple-element.32) | copy-start | bytes 786436
  354.2 74.6 %copy-start.6 = (bf16[1,16,64,128]{3,2,1,0:T(8,128)(2,1)S(1)}, bf16[1,16,64,128]{3,2,1,0:T(8,128)(2,1)}, u32[]{:S(2)}) copy-start(bf16[1,16,64,128]{3,2,1,0:T(8,128)(2,1)} %get-tuple-element.33) | copy-start | bytes 786436
  426.4 72.1 %copy-start.14 = (bf16[2,2048,256]{2,1,0:T(8,128)(2,1)S(1)}, bf16[2,2048,256]{2,1,0:T(8,128)(2,1)}, u32[]{:S(2)}) copy-start(bf16[2,2048,256]{2,1,0:T(8,128)(2,1)} %param.21) | copy-start | bytes 6291460
Sparse Core Ops, SparseCore 0:
  166.0 69.6 all-reduce.10
  428.8 69.5 all-reduce.8
